TPU v7x, 256 devices: a whole 4x4x8 slice. The times are simulated.
256 devices in a mesh: tm: 64 (over z, y, core), head: 4 (over x).
Axes of the slice: x: 4, y: 4, z: 8, core: 2. Of those that a mesh axis runs over, the one named last changes fastest.
Arguments:
- tokens: bfloat16 [65536, 2048], P(('tm', 'head')), may hold values from -6 to 6
- frame_counts: int32 [512], P('tm'), may hold values from 1 to 128, 32768 in all
- decay_log: float32 [16, 65536], P('head', 'tm'), may hold values from -3 to 0
- norm_gain: float32 [2048], replicated, may hold values from 0.1 to 1.9
- w_qkv: bfloat16 [2048, 3, 2048], P(None, None, 'head'), may hold values from -0.125 to 0.125
- head_gain: float32 [2048], P('head'), may hold values from 0.1 to 1.9
- w_out: bfloat16 [2048, 2048], P('head'), may hold values from -0.125 to 0.125
Outputs:
- mixed: bfloat16 [65536, 2048], P(('tm', 'head'))
Inputs may be any that keep to these rules, and one draw needn't show every extreme that they name: `frame_counts`: the counts of all 512 frames add up to 32768.
All inputs are finite; a program needn't handle non-finite values. No bound on the sum of `frame_counts` on one device may be relied on, other than what follows from the above.
Results may differ from a plain program's by a relative error of at most 0.0074.
Values may be sent and summed in bfloat16 or wider, within the bound.
A program may use at most 128 MiB of HBM per device.

v0:
```python
import functools

import jax
import jax.numpy as jnp
from jax import lax
from jax.experimental import pallas as pl
from jax.experimental.pallas import tpu as pltpu
from jax.sharding import PartitionSpec as P

MESH = pl.DeviceIdType.MESH
F32 = jnp.float32
BF16 = jnp.bfloat16

FCAP = 128
HD = 128
NX = 4
NP = 8
TM, HEAD = "tm", "head"


def _dot(a, b):
    return jnp.dot(a, b, preferred_element_type=F32)


def _dot_nt(a, b):
    return lax.dot_general(a, b, (((1,), (1,)), ((), ())), preferred_element_type=F32)


def _dot_tn(a, b):
    return lax.dot_general(a, b, (((0,), (0,)), ((), ())), preferred_element_type=F32)


def kernel(
    nz, counts, tok, decay, ngain, hgain, w3, wo, out,
    xall, nrm, wq, qkv, ins, wg, acc, crow, ccb, liveb, dec, ngv, hgv,
    st_acc, st_send, st_recv, inner, pl_send, pl_recv, tot_send, tot_recv,
    pt_send, pt_recv, pr_send, prior, ho_s, ho_r, relay, lsem, ssem, rsem,
):
    rows = xall.shape[1]
    half = rows // 2
    cap = NX * rows
    width = xall.shape[2]
    inn = hgv.shape[1]
    nh = inn // HD
    piece = st_send.shape[1]
    wrow = inn // (nz * NP // 2)
    wcol = width // 2

    tm = lax.axis_index(TM)
    x = lax.axis_index(HEAD)
    z = tm // NP
    p = lax.rem(tm, NP)
    y = p // 2
    core = lax.rem(p, 2)
    xr, xo, xl = lax.rem(x + 1, NX), lax.rem(x + 2, NX), lax.rem(x + 3, NX)

    def plane(d):
        return lax.rem(p + d, NP)

    def zed(d):
        return lax.rem(z + d + nz, nz)

    loads = [
        pltpu.make_async_copy(decay, dec, lsem.at[0]),
        pltpu.make_async_copy(tok, xall.at[x], lsem.at[1]),
        pltpu.make_async_copy(ngain, ngv, lsem.at[2]),
        pltpu.make_async_copy(hgain, hgv, lsem.at[3]),
        pltpu.make_async_copy(w3, wq, lsem.at[4]),
        pltpu.make_async_copy(wo, wg.at[0], lsem.at[5]),
    ]
    for c in loads:
        c.start()

    barrier = pltpu.get_barrier_semaphore()
    for d in range(1, NX):
        pl.semaphore_signal(barrier, inc=1, device_id=(tm, lax.rem(x + d, NX)), device_id_type=MESH)
    for d in range(1, NP):
        pl.semaphore_signal(barrier, inc=1, device_id=(z * NP + plane(d), x), device_id_type=MESH)
    for d in range(1, nz):
        pl.semaphore_signal(barrier, inc=1, device_id=(zed(d) * NP + p, x), device_id_type=MESH)
    pl.semaphore_wait(barrier, NX - 1 + NP - 1 + nz - 1)

    counter = [0]
    started, by_core, slots = [], ([], []), {}

    def remote(src, dst, dev, who=None):
        i = counter[0]
        counter[0] += 1
        c = pltpu.make_async_remote_copy(
            src_ref=src, dst_ref=dst, send_sem=ssem.at[i], recv_sem=rsem.at[i],
            device_id=dev, device_id_type=MESH,
        )
        (started if who is None else by_core[who]).append(c)
        slots[id(c)] = (i, dev)
        return c

    def landing(c, dst):
        i, dev = slots[id(c)]
        return pltpu.make_async_remote_copy(
            src_ref=dst, dst_ref=dst, send_sem=ssem.at[i], recv_sem=rsem.at[i],
            device_id=dev, device_id_type=MESH,
        )

    right, left = (tm, xr), (tm, xl)
    top, bot = pl.ds(0, half), pl.ds(half, half)

    ny = NP // 2
    wcols = pl.ds(pl.multiple_of(core * wcol, wcol), wcol)
    wr0 = pl.multiple_of(((1 - core) * (z * ny + y) + core * (y * nz + z)) * wrow, wrow)
    wx = []
    for d in range(1, NX):
        c = remote(
            wo.at[pl.ds(wr0, wrow), wcols], wg.at[NX - d, pl.ds(wr0, wrow), wcols],
            (tm, lax.rem(x + d, NX)),
        )
        c.start()
        wx.append(landing(c, wg.at[NX - d, pl.ds(wr0, wrow), wcols]))

    q0, q1, q2, q3 = [pl.ds(i * (half // 2), half // 2) for i in range(4)]
    ag_ra = remote(tok.at[top], xall.at[x, top], right)
    ag_lb = remote(tok.at[bot], xall.at[x, bot], left)
    ag_rb = remote(tok.at[bot], xall.at[x, bot], right)
    ag_la = remote(tok.at[top], xall.at[x, top], left)
    for c in (ag_ra, ag_lb, ag_rb, ag_la):
        c.start()
    ag_fr = [remote(xall.at[xl, q], xall.at[xl, q], right) for q in (q1, q0)]
    ag_fl = [remote(xall.at[xr, q], xall.at[xr, q], left) for q in (q2, q3)]
    in_la = landing(ag_ra, xall.at[xl, top])
    in_rb = landing(ag_lb, xall.at[xr, bot])
    in_lb = landing(ag_rb, xall.at[xl, bot])
    in_ra = landing(ag_la, xall.at[xr, top])
    in_oa = [landing(c, xall.at[xo, q]) for c, q in zip(ag_fr, (q1, q0))]
    in_ob = [landing(c, xall.at[xo, q]) for c, q in zip(ag_fl, (q2, q3))]

    loads[0].wait()
    lane = lax.broadcasted_iota(jnp.int32, (nh, FCAP), 1)
    sub = lax.broadcasted_iota(jnp.int32, (FCAP, HD), 0)
    parts = []
    for f in range(cap // FCAP):
        n = counts[f]
        parts.append(jnp.where(lane < n, dec[:, f * FCAP:(f + 1) * FCAP], 0.0))
        liveb[f * FCAP:(f + 1) * FCAP, :] = jnp.where(sub < n, 1.0, 0.0)
    run = jnp.concatenate(parts, axis=1)
    at = lax.broadcasted_iota(jnp.int32, (nh, cap), 1)
    k = 1
    while k < cap:
        run = run + jnp.where(at >= k, pltpu.roll(run, k, axis=1), 0.0)
        k *= 2
    crow[...] = run
    for h in range(nh):
        def spread(b, _, h=h):
            at_b = pl.ds(pl.multiple_of(b * HD, HD), HD)
            ccb[h, at_b, :] = jnp.broadcast_to(crow[h:h + 1, at_b], (HD, HD)).T
            return 0
        lax.fori_loop(0, cap // HD, spread, 0)
    tot_send[...] = jnp.concatenate([ccb[h % nh, cap - 1:cap, :] for h in range(8)], axis=0)

    tot = []
    for d in range(1, NP):
        c = remote(tot_send, tot_recv.at[p], (z * NP + plane(d), x))
        c.start()
        tot.append(landing(c, tot_recv.at[plane(NP - d)]))
    tot_recv[p] = tot_send[...]

    ext = pl.ds(1, NX - 1)
    cols0, cols1 = pl.ds(0, wcol), pl.ds(wcol, wcol)
    sibling = (z * NP + y * 2 + (1 - core), x)

    def yed(d):
        return lax.rem(y + d + ny, ny)

    def at_y(d):
        return (z * NP + yed(d) * 2 + core, x)

    def at_z(d):
        return (zed(d) * NP + p, x)

    def piece0(zb, yb):
        return wg.at[ext, pl.ds(pl.multiple_of((zb * ny + yb) * wrow, wrow), wrow), cols0]

    def piece1(zb, yb):
        return wg.at[ext, pl.ds(pl.multiple_of((yb * nz + zb) * wrow, wrow), wrow), cols1]

    def block0(zb):
        return wg.at[ext, pl.ds(pl.multiple_of(zb * (ny * wrow), ny * wrow), ny * wrow), cols0]

    def block1(yb, part=None):
        n = nz * wrow
        r = yb * n
        if part is not None:
            n = n // 2
            r = r + part * n
        return wg.at[ext, pl.ds(pl.multiple_of(r, n), n), cols1]

    ups, downs = nz // 2, (nz - 1) // 2
    wy = [remote(piece0(z, y), piece0(z, y), at_y(d), 0) for d in range(1, ny)]
    wy_in = [landing(c, piece0(z, yed(-d - 1))) for d, c in enumerate(wy)]
    up = [remote(block0(zed(-s)), block0(zed(-s)), at_z(1), 0) for s in range(ups)]
    down = [remote(block0(zed(s)), block0(zed(s)), at_z(-1), 0) for s in range(downs)]
    up_in = [landing(c, block0(zed(-s - 1))) for s, c in enumerate(up)]
    down_in = [landing(c, block0(zed(s + 1))) for s, c in enumerate(down)]
    cross0 = {s: remote(block0(zed(s)), block0(zed(s)), sibling, 0) for s in range(-ups, downs + 1)}
    cross0_in = [landing(c, block0(zed(s))) for s, c in cross0.items()]

    wz = [remote(piece1(z, y), piece1(z, y), at_z(d), 1) for d in range(1, nz)]
    wz_in = [landing(c, piece1(zed(-d - 1), y)) for d, c in enumerate(wz)]
    ring_r = remote(block1(y), block1(y), at_y(1), 1)
    ring_l = remote(block1(y), block1(y), at_y(-1), 1)
    ring_r_in = landing(ring_r, block1(yed(-1)))
    ring_l_in = landing(ring_l, block1(yed(1)))
    pass_r = remote(block1(yed(-1), 0), block1(yed(-1), 0), at_y(1), 1)
    pass_l = remote(block1(yed(1), 1), block1(yed(1), 1), at_y(-1), 1)
    pass_r_in = landing(pass_r, block1(yed(2), 0))
    pass_l_in = landing(pass_l, block1(yed(2), 1))
    cross1 = {s: remote(block1(yed(s)), block1(yed(s)), sibling, 1) for s in (0, -1, 1, 2)}
    cross1_in = [landing(c, block1(yed(s))) for s, c in cross1.items()]

    def relay_w(s):
        if s == 0:
            for c in wy_in:
                c.wait_recv()
            cross0[0].start()
        else:
            up_in[s - 1].wait_recv()
            if s < ups:
                up[s].start()
            cross0[-s].start()
            if s <= downs:
                down_in[s - 1].wait_recv()
                cross0[s].start()
        if s == 0:
            up[0].start()
        if s < downs:
            down[s].start()

    for c in wx:
        c.wait_recv()

    @pl.when(core == 0)
    def _():
        for c in wy:
            c.start()

    @pl.when(core == 1)
    def _():
        for c in wz:
            c.start()

    pt = []
    for d in range(1, nz):
        c = remote(pt_send, pt_recv.at[z], at_z(d))
        pt.append((c, landing(c, pt_recv.at[zed(-d)])))

    st_acc[...] = jnp.zeros_like(st_acc)
    seg = half // 2

    def unit(u, _):
        @pl.when(u == 0)
        def _():
            loads[1].wait()
            loads[2].wait()
            loads[4].wait()

        @pl.when(u == 2)
        def _():
            @pl.when(core == 0)
            def _():
                relay_w(0)

            in_la.wait_recv()
            for c in ag_fr:
                c.start()
            in_rb.wait_recv()
            for c in ag_fl:
                c.start()

            @pl.when(core == 1)
            def _():
                for c in wz_in:
                    c.wait_recv()
                ring_r.start()
                ring_l.start()
                cross1[0].start()

            for c in tot:
                c.wait_recv()
            total = tot_recv[0]
            for j in range(1, NP):
                total = total + tot_recv[j]
            pt_send[...] = total
            pt_recv[z] = total
            for c, _ in pt:
                c.start()

        @pl.when((u == 3) & (core == 0))
        def _():
            relay_w(1)

        @pl.when(u == 4)
        def _():
            @pl.when(core == 0)
            def _():
                relay_w(2)

            in_lb.wait_recv()

        @pl.when(u == 5)
        def _():
            in_ra.wait_recv()

        @pl.when(u == 6)
        def _():
            @pl.when(core == 0)
            def _():
                relay_w(3)

            @pl.when(core == 1)
            def _():
                ring_r_in.wait_recv()
                pass_r.start()
                ring_l_in.wait_recv()
                pass_l.start()
                cross1[-1].start()
                cross1[1].start()

            in_oa[0].wait_recv()
            in_ob[0].wait_recv()

        @pl.when(u == 7)
        def _():
            in_oa[1].wait_recv()
            in_ob[1].wait_recv()

        from_left = (u == 2) | (u == 4)
        off = jnp.where(u < 2, 0, jnp.where(u > 5, 2, jnp.where(from_left, 3, 1)))
        ci = lax.rem(x + off, NX)
        low = jnp.where((u == 1) | (u == 3) | (u == 4), 2, jnp.where(u == 6, 1, 0))
        high = jnp.where(u == 7, 3, low + 1)
        step = 32

        for e, sg in enumerate((low, high)):
            def norm(i, _, e=e, sg=sg):
                src = pl.ds(pl.multiple_of(sg * seg + i * step, step), step)
                dst = pl.ds(pl.multiple_of(e * seg + i * step, step), step)
                v = xall[ci, src, :].astype(F32)
                scale = lax.rsqrt(jnp.sum(v * v, axis=1, keepdims=True) * (1.0 / width) + 1e-05)
                nrm[dst, :] = (v * scale * ngv[...]).astype(BF16)
                return 0

            lax.fori_loop(0, seg // step, norm, 0)

        segs = [pl.ds(pl.multiple_of(ci * rows + sg * seg, seg), seg) for sg in (low, high)]
        wide = 256
        for j in (1, 2, 0):
            for n in range(inn // wide):
                cols = slice(n * wide, (n + 1) * wide)
                v = _dot(nrm[...], wq[j, :, cols])
                for e, rs in enumerate(segs):
                    part = v[e * seg:(e + 1) * seg]
                    if j == 1:
                        part = part * jnp.concatenate([liveb[rs, :]] * (wide // HD), axis=1)
                    qkv[j, rs, cols] = part.astype(BF16)

        for h in range(nh):
            cols = slice(h * HD, (h + 1) * HD)
            last_c = ccb[h, cap - 1:cap, :]
            ks, vs = [], []
            for rs in segs:
                ks.append((qkv[1, rs, cols].astype(F32) * jnp.exp(last_c - ccb[h, rs, :])).astype(BF16))
                vs.append(qkv[2, rs, cols])
            st_acc[h] += _dot_tn(jnp.concatenate(ks, axis=0), jnp.concatenate(vs, axis=0))
        return 0

    lax.fori_loop(0, 8, unit, 0)

    per = HD // piece
    st = []
    for d in range(1, NP):
        c = remote(st_send.at[plane(d)], st_recv.at[p], (z * NP + plane(d), x))
        st.append((c, landing(c, st_recv.at[plane(NP - d)])))
    pls = []
    for d in range(1, nz):
        c = remote(pl_send, pl_recv.at[z], (zed(d) * NP + p, x))
        pls.append((c, landing(c, pl_recv.at[zed(-d)])))
    prs = []
    for d in range(1, NP):
        c = remote(pr_send.at[plane(d)], prior.at[p], (z * NP + plane(d), x))
        prs.append((c, landing(c, prior.at[plane(NP - d)])))
    hq = p // per

    for q in range(NP):
        st_send[q] = st_acc[q // per, (q % per) * piece:(q % per + 1) * piece, :].astype(BF16)
    for c, _ in st:
        c.start()
    st_recv[p] = st_send[p]

    tile = 256
    ri = lax.broadcasted_iota(jnp.int32, (tile, tile), 0)
    ci_ = lax.broadcasted_iota(jnp.int32, (tile, tile), 1)

    def inside(h, _):
        cols = pl.ds(pl.multiple_of(h * HD, HD), HD)
        for i in range(cap // tile):
            ra = slice(i * tile, (i + 1) * tile)
            q = qkv[0, ra, cols]
            ccol = ccb[h, ra, :]
            ccol = jnp.concatenate([ccol] * (tile // HD), axis=1)
            o = jnp.zeros((tile, HD), F32)
            for j in range(i + 1):
                sa = slice(j * tile, (j + 1) * tile)
                sc = _dot_nt(q, qkv[1, sa, cols])
                gap = ccol - crow[pl.ds(h, 1), sa]
                if i == j:
                    gap = jnp.where(ri >= ci_, gap, -1e30)
                o = o + _dot((sc * jnp.exp(gap)).astype(BF16), qkv[2, sa, cols])
            ins[ra, cols] = o

        @pl.when(h == 1)
        def _():
            for _, c in st:
                c.wait_recv()
            state = jnp.zeros((piece, HD), F32)
            for j in range(NP):
                inner[j] = state
                state = jnp.exp(tot_recv[j, pl.ds(hq, 1), :]) * state + st_recv[j].astype(F32)
            pl_send[...] = state.astype(BF16)
            for c, _ in pls:
                c.start()
            pl_recv[z] = pl_send[...]

        @pl.when(h == 2)
        def _():
            @pl.when(core == 0)
            def _():
                relay_w(4)

            @pl.when(core == 1)
            def _():
                pass_r_in.wait_recv()
                pass_l_in.wait_recv()
                cross1[2].start()

            for _, c in pt:
                c.wait_recv()
            for _, c in pls:
                c.wait_recv()
            state = jnp.zeros((piece, HD), F32)
            for j in range(nz):
                nxt = jnp.exp(pt_recv[j, pl.ds(hq, 1), :]) * state + pl_recv[j].astype(F32)
                state = jnp.where(j < z, nxt, state)
            seen = jnp.zeros((1, HD), F32)
            for j in range(NP):
                pr_send[j] = (inner[j] + jnp.exp(seen) * state).astype(BF16)
                seen = seen + tot_recv[j, pl.ds(hq, 1), :]
            for c, _ in prs:
                c.start()
            prior[p] = pr_send[p]
        return 0

    lax.fori_loop(0, nh, inside, 0)

    a2a_oa = remote(ho_s.at[2, top], relay.at[0], right)
    a2a_ob = remote(ho_s.at[2, bot], relay.at[1], left)
    a2a_r = remote(ho_s.at[1], ho_r.at[3], right)
    a2a_l = remote(ho_s.at[3], ho_r.at[1], left)
    a2a_fr = remote(relay.at[0], ho_r.at[2, top], right)
    a2a_fl = remote(relay.at[1], ho_r.at[2, bot], left)
    got_oa = landing(a2a_oa, relay.at[0])
    got_ob = landing(a2a_ob, relay.at[1])
    got_l = landing(a2a_r, ho_r.at[3])
    got_r = landing(a2a_l, ho_r.at[1])
    got_fa = landing(a2a_fr, ho_r.at[2, top])
    got_fb = landing(a2a_fl, ho_r.at[2, bot])

    loads[3].wait()
    for _, c in prs:
        c.wait_recv()

    def attended(s, _):
        off = jnp.where(s == 0, 2, jnp.where(s == 1, 1, jnp.where(s == 2, 3, 0)))
        r0 = pl.multiple_of(lax.rem(x + off, NX) * rows, rows)
        ra = pl.ds(r0, rows)
        for h in range(nh):
            cols = slice(h * HD, (h + 1) * HD)
            held = jnp.concatenate([prior[h * per + e] for e in range(per)], axis=0)
            o = ins[ra, cols] + _dot(qkv[0, ra, cols], held) * jnp.exp(ccb[h, ra, :])
            r = lax.rsqrt(jnp.sum(o * o, axis=1, keepdims=True) * (1.0 / HD) + 1e-05)
            ho_s[off, :, cols] = (o * r * hgv[:, cols]).astype(BF16)

        @pl.when(s == 0)
        def _():
            a2a_oa.start()
            a2a_ob.start()

        @pl.when(s == 1)
        def _():
            a2a_r.start()

        @pl.when(s == 2)
        def _():
            a2a_l.start()

        return 0

    lax.fori_loop(0, NX, attended, 0)
    got_oa.wait_recv()
    a2a_fr.start()
    got_ob.wait_recv()
    a2a_fl.start()

    loads[5].wait()
    wide = 512
    own = pl.multiple_of(x * rows, rows)
    lv = liveb[pl.ds(own, rows), :]
    lv = jnp.concatenate([lv] * (wide // HD), axis=1)

    def first(n, _):
        cols = pl.ds(pl.multiple_of(n * wide, wide), wide)
        acc[:, cols] = _dot(ho_s[0], wg[0, :, cols]) + xall[x, :, cols].astype(F32)
        return 0

    lax.fori_loop(0, width // wide, first, 0)

    @pl.when(core == 1)
    def _():
        for c in cross0_in:
            c.wait_recv()

    @pl.when(core == 0)
    def _():
        for c in cross1_in:
            c.wait_recv()

    def more(i, _):
        @pl.when(i == 0)
        def _():
            got_l.wait_recv()

        @pl.when(i == 1)
        def _():
            got_r.wait_recv()

        q = jnp.where(i == 0, 3, 1)

        def col(n, _):
            cols = pl.ds(pl.multiple_of(n * wide, wide), wide)
            acc[:, cols] += _dot(ho_r[q], wg[q, :, cols])
            return 0

        lax.fori_loop(0, width // wide, col, 0)
        return 0

    lax.fori_loop(0, 2, more, 0)
    got_fa.wait_recv()
    got_fb.wait_recv()

    def last(n, _):
        cols = pl.ds(pl.multiple_of(n * wide, wide), wide)
        v = acc[:, cols] + _dot(ho_r[2], wg[2, :, cols])
        out[:, cols] = (v * lv).astype(BF16)
        return 0

    lax.fori_loop(0, width // wide, last, 0)
    for c in started:
        c.wait_send()
    for who in range(2):
        @pl.when(core == who)
        def _(who=who):
            for c in by_core[who]:
                c.wait_send()


def on_device(tokens, frame_counts, decay_log, norm_gain, w_qkv, head_gain, w_out, *, nz):
    rows, width = tokens.shape
    inn = w_qkv.shape[2]
    nh = inn // HD
    cap = NX * rows
    piece = nh * HD // NP
    n_sem = 96
    vm = pltpu.VMEM
    anyspace = pl.BlockSpec(memory_space=pl.ANY)
    return pl.pallas_call(
        functools.partial(kernel, nz),
        out_shape=pltpu.VMEM((rows, width), BF16),
        in_specs=[pl.BlockSpec(memory_space=pltpu.SMEM)] + [anyspace] * 6,
        out_specs=pl.BlockSpec(memory_space=pltpu.VMEM),
        scratch_shapes=[
            vm((NX, rows, width), BF16),
            vm((rows // 2, width), BF16),
            vm((3, width, inn), BF16),
            vm((3, cap, inn), BF16),
            vm((cap, inn), F32),
            vm((NX, inn, width), BF16),
            vm((rows, width), F32),
            vm((nh, cap), F32),
            vm((nh, cap, HD), F32),
            vm((cap, HD), F32),
            vm((nh, cap), F32),
            vm((1, width), F32),
            vm((1, inn), F32),
            vm((nh, HD, HD), F32),
            vm((NP, piece, HD), BF16),
            vm((NP, piece, HD), BF16),
            vm((NP, piece, HD), F32),
            vm((piece, HD), BF16),
            vm((nz, piece, HD), BF16),
            vm((8, HD), F32),
            vm((NP, 8, HD), F32),
            vm((8, HD), F32),
            vm((nz, 8, HD), F32),
            vm((NP, piece, HD), BF16),
            vm((NP, piece, HD), BF16),
            vm((NX, rows, inn), BF16),
            vm((NX, rows, inn), BF16),
            vm((2, rows // 2, inn), BF16),
            pltpu.SemaphoreType.DMA((6,)),
            pltpu.SemaphoreType.DMA((n_sem,)),
            pltpu.SemaphoreType.DMA((n_sem,)),
        ],
        compiler_params=pltpu.CompilerParams(collective_id=0, has_side_effects=True),
        name="sublayer",
    )(
        frame_counts,
        tokens,
        decay_log,
        norm_gain.reshape(1, width),
        head_gain.reshape(1, inn),
        jnp.transpose(w_qkv, (1, 0, 2)),
        w_out,
    )


def solution(mesh):
    nz = mesh.shape[TM] // NP
    return jax.shard_map(
        functools.partial(on_device, nz=nz),
        mesh=mesh,
        in_specs=(
            P((TM, HEAD), None),
            P(TM),
            P(HEAD, TM),
            P(),
            P(None, None, HEAD),
            P(HEAD),
            P(HEAD, None),
        ),
        out_specs=P((TM, HEAD), None),
        check_vma=False,
    )
```

profile of v0, /device:TPU:1, one launch (start us, length us, event | category | flops | bytes accessed | tf_op | source)
XLA Modules:
  0.0 80.6 jit_solution(495010808411084441)
XLA Ops:
  0.0 79.6 %sublayer.1 = bf16[256,2048]{1,0:T(8,128)(2,1)S(1)} custom-call(s32[8]{0:T(128)} %counts.1, bf16[256,2048]{1,0:T(8,128)(2,1)} %tok.1, f32[4,1024]{1,0:T(4,128)} %decay.1, f32[1,2048]{1,0:T(1,128)} %bitcast.4, f32[1,512]{1,0:T(1,128)} %bitcast.5, bf16[3,2048,512]{2,1,0:T(8,128)(2,1)} %bitcast.3, bf16[512,2048]{1,0:T(8,128)(2,1)} %wo.1), custom_call_target="tpu_custom_call" | custom-call | tf_op jit(solution)/shard_map/sublayer/pallas_call | solution.py:582
  79.6 1.0 %copy.9 = bf16[256,2048]{1,0:T(8,128)(2,1)} copy(bf16[256,2048]{1,0:T(8,128)(2,1)S(1)} %sublayer.1) | data formatting | bytes 2097152
where the time goes:
time: 80.7 us; the launch traced here: 80.6 us
  Pallas kernels  79.6 us (99%)
  local copies, waits for them, and re-layouts  0.97 us (1%)
    pallas_call x1, Pallas kernels, on_device(): pl.pallas_call(functools.partial(kernel, nz), out_shape=pltpu.VMEM((rows,...  79.6 us

commit v1 on v0

--- a/solution.py
+++ b/solution.py
@@ -80,26 +80,22 @@
         pl.semaphore_signal(barrier, inc=1, device_id=(zed(d) * NP + p, x), device_id_type=MESH)
     pl.semaphore_wait(barrier, NX - 1 + NP - 1 + nz - 1)
 
-    counter = [0]
-    started, by_core, slots = [], ([], []), {}
-
-    def remote(src, dst, dev, who=None):
-        i = counter[0]
-        counter[0] += 1
-        c = pltpu.make_async_remote_copy(
-            src_ref=src, dst_ref=dst, send_sem=ssem.at[i], recv_sem=rsem.at[i],
+    def remote(src, dst, dev, to_send, to_recv):
+        return pltpu.make_async_remote_copy(
+            src_ref=src, dst_ref=dst, send_sem=ssem.at[to_send], recv_sem=rsem.at[to_recv],
             device_id=dev, device_id_type=MESH,
         )
-        (started if who is None else by_core[who]).append(c)
-        slots[id(c)] = (i, dev)
-        return c
-
-    def landing(c, dst):
-        i, dev = slots[id(c)]
-        return pltpu.make_async_remote_copy(
-            src_ref=dst, dst_ref=dst, send_sem=ssem.at[i], recv_sem=rsem.at[i],
-            device_id=dev, device_id_type=MESH,
-        )
+
+    def arrived(ref, to_recv):
+        remote(ref, ref, (tm, x), 0, to_recv).wait_recv()
+
+    def sent(ref, to_send):
+        remote(ref, ref, (tm, x), to_send, 0).wait_send()
+
+    S_WX, S_AG, S_PASS, S_TOT, S_PT, S_ST, S_PL, S_PR, S_OPP, S_NBR, S_FWD, S_W = range(12)
+    R_WX, R_LA, R_RB, R_LB, R_RA, R_O, _, R_TOT, R_PT, R_ST, R_PL, R_PR, R_OA, R_OB, R_L, R_R = range(16)
+    R_F, R_CROSS, R_W = 16, 18, 19
+    FAR = (4, 3, 5, 2, 6, 1, 7)
 
     right, left = (tm, xr), (tm, xl)
     top, bot = pl.ds(0, half), pl.ds(half, half)
@@ -107,30 +103,19 @@
     ny = NP // 2
     wcols = pl.ds(pl.multiple_of(core * wcol, wcol), wcol)
     wr0 = pl.multiple_of(((1 - core) * (z * ny + y) + core * (y * nz + z)) * wrow, wrow)
-    wx = []
     for d in range(1, NX):
-        c = remote(
+        remote(
             wo.at[pl.ds(wr0, wrow), wcols], wg.at[NX - d, pl.ds(wr0, wrow), wcols],
-            (tm, lax.rem(x + d, NX)),
-        )
-        c.start()
-        wx.append(landing(c, wg.at[NX - d, pl.ds(wr0, wrow), wcols]))
+            (tm, lax.rem(x + d, NX)), S_WX, R_WX,
+        ).start()
 
     q0, q1, q2, q3 = [pl.ds(i * (half // 2), half // 2) for i in range(4)]
-    ag_ra = remote(tok.at[top], xall.at[x, top], right)
-    ag_lb = remote(tok.at[bot], xall.at[x, bot], left)
-    ag_rb = remote(tok.at[bot], xall.at[x, bot], right)
-    ag_la = remote(tok.at[top], xall.at[x, top], left)
-    for c in (ag_ra, ag_lb, ag_rb, ag_la):
-        c.start()
-    ag_fr = [remote(xall.at[xl, q], xall.at[xl, q], right) for q in (q1, q0)]
-    ag_fl = [remote(xall.at[xr, q], xall.at[xr, q], left) for q in (q2, q3)]
-    in_la = landing(ag_ra, xall.at[xl, top])
-    in_rb = landing(ag_lb, xall.at[xr, bot])
-    in_lb = landing(ag_rb, xall.at[xl, bot])
-    in_ra = landing(ag_la, xall.at[xr, top])
-    in_oa = [landing(c, xall.at[xo, q]) for c, q in zip(ag_fr, (q1, q0))]
-    in_ob = [landing(c, xall.at[xo, q]) for c, q in zip(ag_fl, (q2, q3))]
+    remote(tok.at[top], xall.at[x, top], right, S_AG, R_LA).start()
+    remote(tok.at[bot], xall.at[x, bot], left, S_AG, R_RB).start()
+    remote(tok.at[bot], xall.at[x, bot], right, S_AG, R_LB).start()
+    remote(tok.at[top], xall.at[x, top], left, S_AG, R_RA).start()
+    pass_right = [remote(xall.at[xl, q], xall.at[xl, q], right, S_PASS, R_O + i) for i, q in enumerate((q1, q0))]
+    pass_left = [remote(xall.at[xr, q], xall.at[xr, q], left, S_PASS, R_O + i) for i, q in enumerate((q2, q3))]
 
     loads[0].wait()
     lane = lax.broadcasted_iota(jnp.int32, (nh, FCAP), 1)
@@ -155,11 +140,8 @@
         lax.fori_loop(0, cap // HD, spread, 0)
     tot_send[...] = jnp.concatenate([ccb[h % nh, cap - 1:cap, :] for h in range(8)], axis=0)
 
-    tot = []
-    for d in range(1, NP):
-        c = remote(tot_send, tot_recv.at[p], (z * NP + plane(d), x))
-        c.start()
-        tot.append(landing(c, tot_recv.at[plane(NP - d)]))
+    for d in FAR:
+        remote(tot_send, tot_recv.at[p], (z * NP + plane(d), x), S_TOT, R_TOT).start()
     tot_recv[p] = tot_send[...]
 
     ext = pl.ds(1, NX - 1)
@@ -193,48 +175,37 @@
         return wg.at[ext, pl.ds(pl.multiple_of(r, n), n), cols1]
 
     ups, downs = nz // 2, (nz - 1) // 2
-    wy = [remote(piece0(z, y), piece0(z, y), at_y(d), 0) for d in range(1, ny)]
-    wy_in = [landing(c, piece0(z, yed(-d - 1))) for d, c in enumerate(wy)]
-    up = [remote(block0(zed(-s)), block0(zed(-s)), at_z(1), 0) for s in range(ups)]
-    down = [remote(block0(zed(s)), block0(zed(s)), at_z(-1), 0) for s in range(downs)]
-    up_in = [landing(c, block0(zed(-s - 1))) for s, c in enumerate(up)]
-    down_in = [landing(c, block0(zed(s + 1))) for s, c in enumerate(down)]
-    cross0 = {s: remote(block0(zed(s)), block0(zed(s)), sibling, 0) for s in range(-ups, downs + 1)}
-    cross0_in = [landing(c, block0(zed(s))) for s, c in cross0.items()]
-
-    wz = [remote(piece1(z, y), piece1(z, y), at_z(d), 1) for d in range(1, nz)]
-    wz_in = [landing(c, piece1(zed(-d - 1), y)) for d, c in enumerate(wz)]
-    ring_r = remote(block1(y), block1(y), at_y(1), 1)
-    ring_l = remote(block1(y), block1(y), at_y(-1), 1)
-    ring_r_in = landing(ring_r, block1(yed(-1)))
-    ring_l_in = landing(ring_l, block1(yed(1)))
-    pass_r = remote(block1(yed(-1), 0), block1(yed(-1), 0), at_y(1), 1)
-    pass_l = remote(block1(yed(1), 1), block1(yed(1), 1), at_y(-1), 1)
-    pass_r_in = landing(pass_r, block1(yed(2), 0))
-    pass_l_in = landing(pass_l, block1(yed(2), 1))
-    cross1 = {s: remote(block1(yed(s)), block1(yed(s)), sibling, 1) for s in (0, -1, 1, 2)}
-    cross1_in = [landing(c, block1(yed(s))) for s, c in cross1.items()]
+    zfar = sorted(range(1, nz), key=lambda d: -min(d, nz - d))
+    wy = [remote(piece0(z, y), piece0(z, y), at_y(d), S_W, R_W) for d in (2, 1, 3)]
+    up = [remote(block0(zed(-s)), block0(zed(-s)), at_z(1), S_W + 1, R_W + 1 + s) for s in range(ups)]
+    down = [remote(block0(zed(s)), block0(zed(s)), at_z(-1), S_W + 1, R_W + 1 + s) for s in range(downs)]
+    cross0 = {s: remote(block0(zed(s)), block0(zed(s)), sibling, S_W + 2, R_CROSS) for s in range(-ups, downs + 1)}
+
+    wz = [remote(piece1(z, y), piece1(z, y), at_z(d), S_W, R_W) for d in zfar]
+    ring = [remote(block1(y), block1(y), at_y(d), S_W + 1, R_W + 1) for d in (1, -1)]
+    ring_on = [
+        remote(block1(yed(-1), 0), block1(yed(-1), 0), at_y(1), S_W + 2, R_W + 2),
+        remote(block1(yed(1), 1), block1(yed(1), 1), at_y(-1), S_W + 2, R_W + 2),
+    ]
+    cross1 = {s: remote(block1(yed(s)), block1(yed(s)), sibling, S_W + 3, R_CROSS) for s in (0, -1, 1, 2)}
+
+    def wpart(n, cols):
+        return wg.at[ext, pl.ds(0, n * wrow), cols]
 
     def relay_w(s):
         if s == 0:
-            for c in wy_in:
-                c.wait_recv()
-            cross0[0].start()
+            arrived(wpart(ny - 1, cols0), R_W)
         else:
-            up_in[s - 1].wait_recv()
-            if s < ups:
-                up[s].start()
-            cross0[-s].start()
-            if s <= downs:
-                down_in[s - 1].wait_recv()
-                cross0[s].start()
-        if s == 0:
-            up[0].start()
+            arrived(wpart(ny * (2 if s <= downs else 1), cols0), R_W + s)
+        if s < ups:
+            up[s].start()
         if s < downs:
             down[s].start()
-
-    for c in wx:
-        c.wait_recv()
+        cross0[-s].start()
+        if 0 < s <= downs:
+            cross0[s].start()
+
+    arrived(wg.at[ext, pl.ds(0, wrow), wcols], R_WX)
 
     @pl.when(core == 0)
     def _():
@@ -246,10 +217,7 @@
         for c in wz:
             c.start()
 
-    pt = []
-    for d in range(1, nz):
-        c = remote(pt_send, pt_recv.at[z], at_z(d))
-        pt.append((c, landing(c, pt_recv.at[zed(-d)])))
+    pt = [remote(pt_send, pt_recv.at[z], at_z(d), S_PT, R_PT) for d in zfar]
 
     st_acc[...] = jnp.zeros_like(st_acc)
     seg = half // 2
@@ -267,29 +235,27 @@
             def _():
                 relay_w(0)
 
-            in_la.wait_recv()
-            for c in ag_fr:
+            arrived(xall.at[xl, top], R_LA)
+            for c in pass_right:
                 c.start()
-            in_rb.wait_recv()
-            for c in ag_fl:
+            arrived(xall.at[xr, bot], R_RB)
+            for c in pass_left:
                 c.start()
 
             @pl.when(core == 1)
             def _():
-                for c in wz_in:
-                    c.wait_recv()
-                ring_r.start()
-                ring_l.start()
+                arrived(wpart(nz - 1, cols1), R_W)
+                for c in ring:
+                    c.start()
                 cross1[0].start()
 
-            for c in tot:
-                c.wait_recv()
+            arrived(tot_recv.at[pl.ds(0, NP - 1)], R_TOT)
             total = tot_recv[0]
             for j in range(1, NP):
                 total = total + tot_recv[j]
             pt_send[...] = total
             pt_recv[z] = total
-            for c, _ in pt:
+            for c in pt:
                 c.start()
 
         @pl.when((u == 3) & (core == 0))
@@ -302,11 +268,11 @@
             def _():
                 relay_w(2)
 
-            in_lb.wait_recv()
+            arrived(xall.at[xl, bot], R_LB)
 
         @pl.when(u == 5)
         def _():
-            in_ra.wait_recv()
+            arrived(xall.at[xr, top], R_RA)
 
         @pl.when(u == 6)
         def _():
@@ -316,20 +282,17 @@
 
             @pl.when(core == 1)
             def _():
-                ring_r_in.wait_recv()
-                pass_r.start()
-                ring_l_in.wait_recv()
-                pass_l.start()
+                arrived(wpart(2 * nz, cols1), R_W + 1)
+                for c in ring_on:
+                    c.start()
                 cross1[-1].start()
                 cross1[1].start()
 
-            in_oa[0].wait_recv()
-            in_ob[0].wait_recv()
+            arrived(xall.at[xo, top], R_O)
 
         @pl.when(u == 7)
         def _():
-            in_oa[1].wait_recv()
-            in_ob[1].wait_recv()
+            arrived(xall.at[xo, top], R_O + 1)
 
         from_left = (u == 2) | (u == 4)
         off = jnp.where(u < 2, 0, jnp.where(u > 5, 2, jnp.where(from_left, 3, 1)))
@@ -374,23 +337,14 @@
     lax.fori_loop(0, 8, unit, 0)
 
     per = HD // piece
-    st = []
-    for d in range(1, NP):
-        c = remote(st_send.at[plane(d)], st_recv.at[p], (z * NP + plane(d), x))
-        st.append((c, landing(c, st_recv.at[plane(NP - d)])))
-    pls = []
-    for d in range(1, nz):
-        c = remote(pl_send, pl_recv.at[z], (zed(d) * NP + p, x))
-        pls.append((c, landing(c, pl_recv.at[zed(-d)])))
-    prs = []
-    for d in range(1, NP):
-        c = remote(pr_send.at[plane(d)], prior.at[p], (z * NP + plane(d), x))
-        prs.append((c, landing(c, prior.at[plane(NP - d)])))
+    st = [remote(st_send.at[plane(d)], st_recv.at[p], (z * NP + plane(d), x), S_ST, R_ST) for d in FAR]
+    pls = [remote(pl_send, pl_recv.at[z], at_z(d), S_PL, R_PL) for d in zfar]
+    prs = [remote(pr_send.at[plane(d)], prior.at[p], (z * NP + plane(d), x), S_PR, R_PR) for d in FAR]
     hq = p // per
 
     for q in range(NP):
         st_send[q] = st_acc[q // per, (q % per) * piece:(q % per + 1) * piece, :].astype(BF16)
-    for c, _ in st:
+    for c in st:
         c.start()
     st_recv[p] = st_send[p]
 
@@ -417,14 +371,13 @@
 
         @pl.when(h == 1)
         def _():
-            for _, c in st:
-                c.wait_recv()
+            arrived(st_recv.at[pl.ds(0, NP - 1)], R_ST)
             state = jnp.zeros((piece, HD), F32)
             for j in range(NP):
                 inner[j] = state
                 state = jnp.exp(tot_recv[j, pl.ds(hq, 1), :]) * state + st_recv[j].astype(F32)
             pl_send[...] = state.astype(BF16)
-            for c, _ in pls:
+            for c in pls:
                 c.start()
             pl_recv[z] = pl_send[...]
 
@@ -436,14 +389,11 @@
 
             @pl.when(core == 1)
             def _():
-                pass_r_in.wait_recv()
-                pass_l_in.wait_recv()
+                arrived(wpart(nz, cols1), R_W + 2)
                 cross1[2].start()
 
-            for _, c in pt:
-                c.wait_recv()
-            for _, c in pls:
-                c.wait_recv()
+            arrived(pt_recv.at[pl.ds(0, nz - 1)], R_PT)
+            arrived(pl_recv.at[pl.ds(0, nz - 1)], R_PL)
             state = jnp.zeros((piece, HD), F32)
             for j in range(nz):
                 nxt = jnp.exp(pt_recv[j, pl.ds(hq, 1), :]) * state + pl_recv[j].astype(F32)
@@ -452,29 +402,23 @@
             for j in range(NP):
                 pr_send[j] = (inner[j] + jnp.exp(seen) * state).astype(BF16)
                 seen = seen + tot_recv[j, pl.ds(hq, 1), :]
-            for c, _ in prs:
+            for c in prs:
                 c.start()
             prior[p] = pr_send[p]
         return 0
 
     lax.fori_loop(0, nh, inside, 0)
 
-    a2a_oa = remote(ho_s.at[2, top], relay.at[0], right)
-    a2a_ob = remote(ho_s.at[2, bot], relay.at[1], left)
-    a2a_r = remote(ho_s.at[1], ho_r.at[3], right)
-    a2a_l = remote(ho_s.at[3], ho_r.at[1], left)
-    a2a_fr = remote(relay.at[0], ho_r.at[2, top], right)
-    a2a_fl = remote(relay.at[1], ho_r.at[2, bot], left)
-    got_oa = landing(a2a_oa, relay.at[0])
-    got_ob = landing(a2a_ob, relay.at[1])
-    got_l = landing(a2a_r, ho_r.at[3])
-    got_r = landing(a2a_l, ho_r.at[1])
-    got_fa = landing(a2a_fr, ho_r.at[2, top])
-    got_fb = landing(a2a_fl, ho_r.at[2, bot])
+    hcols = [pl.ds(i * (inn // 2), inn // 2) for i in range(2)]
+    a2a_oa = remote(ho_s.at[2, top], relay.at[0], right, S_OPP, R_OA)
+    a2a_ob = remote(ho_s.at[2, bot], relay.at[1], left, S_OPP, R_OB)
+    a2a_r = remote(ho_s.at[1], ho_r.at[3], right, S_NBR, R_L)
+    a2a_l = remote(ho_s.at[3], ho_r.at[1], left, S_NBR, R_R)
+    on_right = [remote(relay.at[0, :, c], ho_r.at[2, top, c], right, S_FWD, R_F + i) for i, c in enumerate(hcols)]
+    on_left = [remote(relay.at[1, :, c], ho_r.at[2, bot, c], left, S_FWD, R_F + i) for i, c in enumerate(hcols)]
 
     loads[3].wait()
-    for _, c in prs:
-        c.wait_recv()
+    arrived(prior.at[pl.ds(0, NP - 1)], R_PR)
 
     def attended(s, _):
         off = jnp.where(s == 0, 2, jnp.where(s == 1, 1, jnp.where(s == 2, 3, 0)))
@@ -503,10 +447,12 @@
         return 0
 
     lax.fori_loop(0, NX, attended, 0)
-    got_oa.wait_recv()
-    a2a_fr.start()
-    got_ob.wait_recv()
-    a2a_fl.start()
+    arrived(relay.at[0], R_OA)
+    for c in on_right:
+        c.start()
+    arrived(relay.at[1], R_OB)
+    for c in on_left:
+        c.start()
 
     loads[5].wait()
     wide = 512
@@ -520,25 +466,16 @@
         return 0
 
     lax.fori_loop(0, width // wide, first, 0)
-
-    @pl.when(core == 1)
-    def _():
-        for c in cross0_in:
-            c.wait_recv()
-
-    @pl.when(core == 0)
-    def _():
-        for c in cross1_in:
-            c.wait_recv()
+    arrived(wg.at[ext, :, pl.ds(0, wcol)], R_CROSS)
 
     def more(i, _):
         @pl.when(i == 0)
         def _():
-            got_l.wait_recv()
+            arrived(ho_r.at[3], R_L)
 
         @pl.when(i == 1)
         def _():
-            got_r.wait_recv()
+            arrived(ho_r.at[1], R_R)
 
         q = jnp.where(i == 0, 3, 1)
 
@@ -551,23 +488,49 @@
         return 0
 
     lax.fori_loop(0, 2, more, 0)
-    got_fa.wait_recv()
-    got_fb.wait_recv()
+    k0, k1 = slice(0, inn // 2), slice(inn // 2, inn)
+    arrived(relay.at[:, :, hcols[0]], R_F)
+
+    def first_half(n, _):
+        cols = pl.ds(pl.multiple_of(n * wide, wide), wide)
+        acc[:, cols] += _dot(ho_r[2, :, k0], wg[2, k0, cols])
+        return 0
+
+    lax.fori_loop(0, width // wide, first_half, 0)
+    arrived(relay.at[:, :, hcols[1]], R_F + 1)
 
     def last(n, _):
         cols = pl.ds(pl.multiple_of(n * wide, wide), wide)
-        v = acc[:, cols] + _dot(ho_r[2], wg[2, :, cols])
+        v = acc[:, cols] + _dot(ho_r[2, :, k1], wg[2, k1, cols])
         out[:, cols] = (v * lv).astype(BF16)
         return 0
 
     lax.fori_loop(0, width // wide, last, 0)
-    for c in started:
-        c.wait_send()
-    for who in range(2):
-        @pl.when(core == who)
-        def _(who=who):
-            for c in by_core[who]:
-                c.wait_send()
+
+    sent(wg.at[ext, pl.ds(0, wrow), wcols], S_WX)
+    sent(xall.at[pl.ds(0, 2)], S_AG)
+    sent(xall.at[0], S_PASS)
+    sent(tot_recv.at[pl.ds(0, NP - 1)], S_TOT)
+    sent(pt_recv.at[pl.ds(0, nz - 1)], S_PT)
+    sent(st_recv.at[pl.ds(0, NP - 1)], S_ST)
+    sent(pl_recv.at[pl.ds(0, nz - 1)], S_PL)
+    sent(prior.at[pl.ds(0, NP - 1)], S_PR)
+    sent(relay, S_OPP)
+    sent(ho_r.at[pl.ds(0, 2)], S_NBR)
+    sent(relay, S_FWD)
+
+    @pl.when(core == 0)
+    def _():
+        sent(wpart(ny - 1, cols0), S_W)
+        sent(wpart((nz - 1) * ny, cols0), S_W + 1)
+        sent(wpart(nz * ny, cols0), S_W + 2)
+
+    @pl.when(core == 1)
+    def _():
+        sent(wpart(nz - 1, cols1), S_W)
+        sent(wpart(2 * nz, cols1), S_W + 1)
+        sent(wpart(nz, cols1), S_W + 2)
+        sent(wpart(nz * ny, cols1), S_W + 3)
 
 
 def on_device(tokens, frame_counts, decay_log, norm_gain, w_qkv, head_gain, w_out, *, nz):
@@ -576,7 +539,6 @@
     nh = inn // HD
     cap = NX * rows
     piece = nh * HD // NP
-    n_sem = 96
     vm = pltpu.VMEM
     anyspace = pl.BlockSpec(memory_space=pl.ANY)
     return pl.pallas_call(
@@ -614,8 +576,8 @@
             vm((NX, rows, inn), BF16),
             vm((2, rows // 2, inn), BF16),
             pltpu.SemaphoreType.DMA((6,)),
-            pltpu.SemaphoreType.DMA((n_sem,)),
-            pltpu.SemaphoreType.DMA((n_sem,)),
+            pltpu.SemaphoreType.DMA((15,)),
+            pltpu.SemaphoreType.DMA((20 + nz // 2,)),
         ],
         compiler_params=pltpu.CompilerParams(collective_id=0, has_side_effects=True),
         name="sublayer",

time: 80.7 us -> 78.9 us (0.978)
  Pallas kernels: 79.6 us -> 77.7 us
    pallas_call x1, Pallas kernels: 79.6 us -> 77.7 us  [on_device(): pl.pallas_call(functools.partial(kernel, nz), out_shape=pltpu.VMEM((rows,...]
where the time goes in v1:
time: 78.9 us; the launch traced here: 78.7 us
  Pallas kernels  77.7 us (98%)
  local copies, waits for them, and re-layouts  0.97 us (1%)
    pallas_call x1, Pallas kernels, on_device(): pl.pallas_call(functools.partial(kernel, nz), out_shape=pltpu.VMEM((rows,...  77.7 us

profile of v1, /device:TPU:1, one launch (start us, length us, event | category | flops | bytes accessed | tf_op | source)
XLA Modules:
  0.0 78.7 jit_solution(16409059276250444252)
XLA Ops:
  0.0 77.7 %sublayer.1 = bf16[256,2048]{1,0:T(8,128)(2,1)S(1)} custom-call(s32[8]{0:T(128)} %counts.1, bf16[256,2048]{1,0:T(8,128)(2,1)} %tok.1, f32[4,1024]{1,0:T(4,128)} %decay.1, f32[1,2048]{1,0:T(1,128)} %bitcast.4, f32[1,512]{1,0:T(1,128)} %bitcast.5, bf16[3,2048,512]{2,1,0:T(8,128)(2,1)} %bitcast.3, bf16[512,2048]{1,0:T(8,128)(2,1)} %wo.1), custom_call_target="tpu_custom_call" | custom-call | tf_op jit(solution)/shard_map/sublayer/pallas_call | solution.py:544
  77.7 1.0 %copy.9 = bf16[256,2048]{1,0:T(8,128)(2,1)} copy(bf16[256,2048]{1,0:T(8,128)(2,1)S(1)} %sublayer.1) | data formatting | bytes 2097152

commit v2 on v1

--- a/solution.py
+++ b/solution.py
@@ -31,9 +31,9 @@
 
 
 def kernel(
-    nz, counts, tok, decay, ngain, hgain, w3, wo, out,
-    xall, nrm, wq, qkv, ins, wg, acc, crow, ccb, liveb, dec, ngv, hgv,
-    st_acc, st_send, st_recv, inner, pl_send, pl_recv, tot_send, tot_recv,
+    nz, cnt, tok, decay, ngain, hgain, w3, wo, out,
+    counts, xall, nrm, wq, qkv, ins, wg, acc, crow, ccb, liveb, dec, ngv, hgv,
+    st_acc, st_send, st_recv, inner, coef, pl_send, pl_recv, tot_send, tot_recv,
     pt_send, pt_recv, pr_send, prior, ho_s, ho_r, relay, lsem, ssem, rsem,
 ):
     rows = xall.shape[1]
@@ -60,6 +60,14 @@
     def zed(d):
         return lax.rem(z + d + nz, nz)
 
+    barrier = pltpu.get_barrier_semaphore()
+    for d in range(1, NX):
+        pl.semaphore_signal(barrier, inc=1, device_id=(tm, lax.rem(x + d, NX)), device_id_type=MESH)
+    for d in range(1, NP):
+        pl.semaphore_signal(barrier, inc=1, device_id=(z * NP + plane(d), x), device_id_type=MESH)
+    for d in range(1, nz):
+        pl.semaphore_signal(barrier, inc=1, device_id=(zed(d) * NP + p, x), device_id_type=MESH)
+
     loads = [
         pltpu.make_async_copy(decay, dec, lsem.at[0]),
         pltpu.make_async_copy(tok, xall.at[x], lsem.at[1]),
@@ -67,17 +75,11 @@
         pltpu.make_async_copy(hgain, hgv, lsem.at[3]),
         pltpu.make_async_copy(w3, wq, lsem.at[4]),
         pltpu.make_async_copy(wo, wg.at[0], lsem.at[5]),
+        pltpu.make_async_copy(cnt, counts, lsem.at[6]),
     ]
     for c in loads:
         c.start()
 
-    barrier = pltpu.get_barrier_semaphore()
-    for d in range(1, NX):
-        pl.semaphore_signal(barrier, inc=1, device_id=(tm, lax.rem(x + d, NX)), device_id_type=MESH)
-    for d in range(1, NP):
-        pl.semaphore_signal(barrier, inc=1, device_id=(z * NP + plane(d), x), device_id_type=MESH)
-    for d in range(1, nz):
-        pl.semaphore_signal(barrier, inc=1, device_id=(zed(d) * NP + p, x), device_id_type=MESH)
     pl.semaphore_wait(barrier, NX - 1 + NP - 1 + nz - 1)
 
     def remote(src, dst, dev, to_send, to_recv):
@@ -93,7 +95,7 @@
         remote(ref, ref, (tm, x), to_send, 0).wait_send()
 
     S_WX, S_AG, S_PASS, S_TOT, S_PT, S_ST, S_PL, S_PR, S_OPP, S_NBR, S_FWD, S_W = range(12)
-    R_WX, R_LA, R_RB, R_LB, R_RA, R_O, _, R_TOT, R_PT, R_ST, R_PL, R_PR, R_OA, R_OB, R_L, R_R = range(16)
+    R_WX, R_LA, R_RB, R_LB, R_RA, R_O, _, R_TOT, R_PT, R_ST, R_PL, R_PR, R_OA, R_OB, R_N, _ = range(16)
     R_F, R_CROSS, R_W = 16, 18, 19
     FAR = (4, 3, 5, 2, 6, 1, 7)
 
@@ -118,6 +120,7 @@
     pass_left = [remote(xall.at[xr, q], xall.at[xr, q], left, S_PASS, R_O + i) for i, q in enumerate((q2, q3))]
 
     loads[0].wait()
+    loads[6].wait()
     lane = lax.broadcasted_iota(jnp.int32, (nh, FCAP), 1)
     sub = lax.broadcasted_iota(jnp.int32, (FCAP, HD), 0)
     parts = []
@@ -219,8 +222,16 @@
 
     pt = [remote(pt_send, pt_recv.at[z], at_z(d), S_PT, R_PT) for d in zfar]
 
+    st = [remote(st_send.at[plane(d)], st_recv.at[p], (z * NP + plane(d), x), S_ST, R_ST) for d in FAR]
+    pls = [remote(pl_send, pl_recv.at[z], at_z(d), S_PL, R_PL) for d in zfar]
+    prs = [remote(pr_send.at[plane(d)], prior.at[p], (z * NP + plane(d), x), S_PR, R_PR) for d in FAR]
+
+
     st_acc[...] = jnp.zeros_like(st_acc)
+    UNITS = 8
     seg = half // 2
+    per = HD // piece
+    hq = p // per
 
     def unit(u, _):
         @pl.when(u == 0)
@@ -257,6 +268,14 @@
             pt_recv[z] = total
             for c in pt:
                 c.start()
+            after = jnp.zeros((1, HD), F32)
+            for j in reversed(range(NP)):
+                coef[j] = jnp.exp(after)
+                after = after + tot_recv[j, pl.ds(hq, 1), :]
+            before = jnp.zeros((1, HD), F32)
+            for j in range(NP):
+                coef[NP + j] = jnp.exp(before)
+                before = before + tot_recv[j, pl.ds(hq, 1), :]
 
         @pl.when((u == 3) & (core == 0))
         def _():
@@ -292,6 +311,11 @@
 
         @pl.when(u == 7)
         def _():
+            arrived(pt_recv.at[pl.ds(0, nz - 1)], R_PT)
+            after = jnp.zeros((1, HD), F32)
+            for j in reversed(range(nz)):
+                coef[2 * NP + j] = jnp.where(j < z, jnp.exp(after), 0.0)
+                after = after + jnp.where(j < z, pt_recv[j, pl.ds(hq, 1), :], 0.0)
             arrived(xall.at[xo, top], R_O + 1)
 
         from_left = (u == 2) | (u == 4)
@@ -310,11 +334,12 @@
                 nrm[dst, :] = (v * scale * ngv[...]).astype(BF16)
                 return 0
 
-            lax.fori_loop(0, seg // step, norm, 0)
+            lax.fori_loop(0, seg // step, norm, 0, unroll=True)
 
         segs = [pl.ds(pl.multiple_of(ci * rows + sg * seg, seg), seg) for sg in (low, high)]
         wide = 256
-        for j in (1, 2, 0):
+
+        def project(j):
             for n in range(inn // wide):
                 cols = slice(n * wide, (n + 1) * wide)
                 v = _dot(nrm[...], wq[j, :, cols])
@@ -324,6 +349,8 @@
                         part = part * jnp.concatenate([liveb[rs, :]] * (wide // HD), axis=1)
                     qkv[j, rs, cols] = part.astype(BF16)
 
+        project(1)
+        project(2)
         for h in range(nh):
             cols = slice(h * HD, (h + 1) * HD)
             last_c = ccb[h, cap - 1:cap, :]
@@ -332,21 +359,19 @@
                 ks.append((qkv[1, rs, cols].astype(F32) * jnp.exp(last_c - ccb[h, rs, :])).astype(BF16))
                 vs.append(qkv[2, rs, cols])
             st_acc[h] += _dot_tn(jnp.concatenate(ks, axis=0), jnp.concatenate(vs, axis=0))
+
+        @pl.when(u == UNITS - 1)
+        def _():
+            for q in range(NP):
+                st_send[q] = st_acc[q // per, (q % per) * piece:(q % per + 1) * piece, :].astype(BF16)
+            for c in st:
+                c.start()
+            st_recv[p] = st_send[p]
+
+        project(0)
         return 0
 
-    lax.fori_loop(0, 8, unit, 0)
-
-    per = HD // piece
-    st = [remote(st_send.at[plane(d)], st_recv.at[p], (z * NP + plane(d), x), S_ST, R_ST) for d in FAR]
-    pls = [remote(pl_send, pl_recv.at[z], at_z(d), S_PL, R_PL) for d in zfar]
-    prs = [remote(pr_send.at[plane(d)], prior.at[p], (z * NP + plane(d), x), S_PR, R_PR) for d in FAR]
-    hq = p // per
-
-    for q in range(NP):
-        st_send[q] = st_acc[q // per, (q % per) * piece:(q % per + 1) * piece, :].astype(BF16)
-    for c in st:
-        c.start()
-    st_recv[p] = st_send[p]
+    lax.fori_loop(0, UNITS, unit, 0)
 
     tile = 256
     ri = lax.broadcasted_iota(jnp.int32, (tile, tile), 0)
@@ -372,14 +397,17 @@
         @pl.when(h == 1)
         def _():
             arrived(st_recv.at[pl.ds(0, NP - 1)], R_ST)
+            terms = [coef[j] * st_recv[j].astype(F32) for j in range(NP)]
+            while len(terms) > 1:
+                terms = [u + v for u, v in zip(terms[::2], terms[1::2])]
+            pl_send[...] = terms[0].astype(BF16)
+            for c in pls:
+                c.start()
+            pl_recv[z] = pl_send[...]
             state = jnp.zeros((piece, HD), F32)
             for j in range(NP):
                 inner[j] = state
                 state = jnp.exp(tot_recv[j, pl.ds(hq, 1), :]) * state + st_recv[j].astype(F32)
-            pl_send[...] = state.astype(BF16)
-            for c in pls:
-                c.start()
-            pl_recv[z] = pl_send[...]
 
         @pl.when(h == 2)
         def _():
@@ -392,16 +420,12 @@
                 arrived(wpart(nz, cols1), R_W + 2)
                 cross1[2].start()
 
-            arrived(pt_recv.at[pl.ds(0, nz - 1)], R_PT)
             arrived(pl_recv.at[pl.ds(0, nz - 1)], R_PL)
-            state = jnp.zeros((piece, HD), F32)
-            for j in range(nz):
-                nxt = jnp.exp(pt_recv[j, pl.ds(hq, 1), :]) * state + pl_recv[j].astype(F32)
-                state = jnp.where(j < z, nxt, state)
-            seen = jnp.zeros((1, HD), F32)
+            terms = [coef[2 * NP + j] * pl_recv[j].astype(F32) for j in range(nz)]
+            while len(terms) > 1:
+                terms = [u + v for u, v in zip(terms[::2], terms[1::2])] + terms[len(terms) // 2 * 2:]
             for j in range(NP):
-                pr_send[j] = (inner[j] + jnp.exp(seen) * state).astype(BF16)
-                seen = seen + tot_recv[j, pl.ds(hq, 1), :]
+                pr_send[j] = (inner[j] + coef[NP + j] * terms[0]).astype(BF16)
             for c in prs:
                 c.start()
             prior[p] = pr_send[p]
@@ -412,41 +436,47 @@
     hcols = [pl.ds(i * (inn // 2), inn // 2) for i in range(2)]
     a2a_oa = remote(ho_s.at[2, top], relay.at[0], right, S_OPP, R_OA)
     a2a_ob = remote(ho_s.at[2, bot], relay.at[1], left, S_OPP, R_OB)
-    a2a_r = remote(ho_s.at[1], ho_r.at[3], right, S_NBR, R_L)
-    a2a_l = remote(ho_s.at[3], ho_r.at[1], left, S_NBR, R_R)
+    a2a_r = [remote(ho_s.at[1, :, c], ho_r.at[3, :, c], right, S_NBR, R_N + i) for i, c in enumerate(hcols)]
+    a2a_l = [remote(ho_s.at[3, :, c], ho_r.at[1, :, c], left, S_NBR, R_N + i) for i, c in enumerate(hcols)]
     on_right = [remote(relay.at[0, :, c], ho_r.at[2, top, c], right, S_FWD, R_F + i) for i, c in enumerate(hcols)]
     on_left = [remote(relay.at[1, :, c], ho_r.at[2, bot, c], left, S_FWD, R_F + i) for i, c in enumerate(hcols)]
 
     loads[3].wait()
     arrived(prior.at[pl.ds(0, NP - 1)], R_PR)
 
-    def attended(s, _):
+    def attended(i, _):
+        s = i // 2
         off = jnp.where(s == 0, 2, jnp.where(s == 1, 1, jnp.where(s == 2, 3, 0)))
-        r0 = pl.multiple_of(lax.rem(x + off, NX) * rows, rows)
-        ra = pl.ds(r0, rows)
+        h0 = pl.multiple_of(lax.rem(i, 2) * half, half)
+        ra = pl.ds(pl.multiple_of(lax.rem(x + off, NX) * rows + h0, half), half)
         for h in range(nh):
             cols = slice(h * HD, (h + 1) * HD)
             held = jnp.concatenate([prior[h * per + e] for e in range(per)], axis=0)
             o = ins[ra, cols] + _dot(qkv[0, ra, cols], held) * jnp.exp(ccb[h, ra, :])
             r = lax.rsqrt(jnp.sum(o * o, axis=1, keepdims=True) * (1.0 / HD) + 1e-05)
-            ho_s[off, :, cols] = (o * r * hgv[:, cols]).astype(BF16)
-
-        @pl.when(s == 0)
+            ho_s[off, pl.ds(h0, half), cols] = (o * r * hgv[:, cols]).astype(BF16)
+
+        @pl.when(i == 0)
         def _():
             a2a_oa.start()
+
+        @pl.when(i == 1)
+        def _():
             a2a_ob.start()
 
-        @pl.when(s == 1)
-        def _():
-            a2a_r.start()
-
-        @pl.when(s == 2)
-        def _():
-            a2a_l.start()
+        @pl.when(i == 3)
+        def _():
+            for c in a2a_r:
+                c.start()
+
+        @pl.when(i == 5)
+        def _():
+            for c in a2a_l:
+                c.start()
 
         return 0
 
-    lax.fori_loop(0, NX, attended, 0)
+    lax.fori_loop(0, 2 * NX, attended, 0)
     arrived(relay.at[0], R_OA)
     for c in on_right:
         c.start()
@@ -468,27 +498,16 @@
     lax.fori_loop(0, width // wide, first, 0)
     arrived(wg.at[ext, :, pl.ds(0, wcol)], R_CROSS)
 
-    def more(i, _):
-        @pl.when(i == 0)
-        def _():
-            arrived(ho_r.at[3], R_L)
-
-        @pl.when(i == 1)
-        def _():
-            arrived(ho_r.at[1], R_R)
-
-        q = jnp.where(i == 0, 3, 1)
-
-        def col(n, _):
+    k0, k1 = slice(0, inn // 2), slice(inn // 2, inn)
+    for i, ks in enumerate((k0, k1)):
+        arrived(ho_r.at[0], R_N + i)
+
+        def both(n, _, ks=ks):
             cols = pl.ds(pl.multiple_of(n * wide, wide), wide)
-            acc[:, cols] += _dot(ho_r[q], wg[q, :, cols])
+            acc[:, cols] += _dot(ho_r[3, :, ks], wg[3, ks, cols]) + _dot(ho_r[1, :, ks], wg[1, ks, cols])
             return 0
 
-        lax.fori_loop(0, width // wide, col, 0)
-        return 0
-
-    lax.fori_loop(0, 2, more, 0)
-    k0, k1 = slice(0, inn // 2), slice(inn // 2, inn)
+        lax.fori_loop(0, width // wide, both, 0)
     arrived(relay.at[:, :, hcols[0]], R_F)
 
     def first_half(n, _):
@@ -544,9 +563,10 @@
     return pl.pallas_call(
         functools.partial(kernel, nz),
         out_shape=pltpu.VMEM((rows, width), BF16),
-        in_specs=[pl.BlockSpec(memory_space=pltpu.SMEM)] + [anyspace] * 6,
+        in_specs=[anyspace] * 7,
         out_specs=pl.BlockSpec(memory_space=pltpu.VMEM),
         scratch_shapes=[
+            pltpu.SMEM(frame_counts.shape, jnp.int32),
             vm((NX, rows, width), BF16),
             vm((rows // 2, width), BF16),
             vm((3, width, inn), BF16),
@@ -564,6 +584,7 @@
             vm((NP, piece, HD), BF16),
             vm((NP, piece, HD), BF16),
             vm((NP, piece, HD), F32),
+            vm((2 * NP + nz, 1, HD), F32),
             vm((piece, HD), BF16),
             vm((nz, piece, HD), BF16),
             vm((8, HD), F32),
@@ -575,7 +596,7 @@
             vm((NX, rows, inn), BF16),
             vm((NX, rows, inn), BF16),
             vm((2, rows // 2, inn), BF16),
-            pltpu.SemaphoreType.DMA((6,)),
+            pltpu.SemaphoreType.DMA((7,)),
             pltpu.SemaphoreType.DMA((15,)),
             pltpu.SemaphoreType.DMA((20 + nz // 2,)),
         ],

time: 78.9 us -> 76.9 us (0.975)
  Pallas kernels: 77.7 us -> 75.8 us
    pallas_call x1, Pallas kernels: 77.7 us -> 75.8 us  [on_device(): pl.pallas_call(functools.partial(kernel, nz), out_shape=pltpu.VMEM((rows,...]
where the time goes in v2:
time: 76.9 us; the launch traced here: 76.8 us
  Pallas kernels  75.8 us (99%)
  local copies, waits for them, and re-layouts  0.97 us (1%)
    pallas_call x1, Pallas kernels, on_device(): pl.pallas_call(functools.partial(kernel, nz), out_shape=pltpu.VMEM((rows,...  75.8 us

profile of v2, /device:TPU:1, one launch (start us, length us, event | category | flops | bytes accessed | tf_op | source)
XLA Modules:
  0.0 76.8 jit_solution(7690696008479837158)
XLA Ops:
  0.0 75.8 %sublayer.1 = bf16[256,2048]{1,0:T(8,128)(2,1)S(1)} custom-call(s32[8]{0:T(128)} %cnt.1, bf16[256,2048]{1,0:T(8,128)(2,1)} %tok.1, f32[4,1024]{1,0:T(4,128)} %decay.1, f32[1,2048]{1,0:T(1,128)} %bitcast.4, f32[1,512]{1,0:T(1,128)} %bitcast.5, bf16[3,2048,512]{2,1,0:T(8,128)(2,1)} %bitcast.3, bf16[512,2048]{1,0:T(8,128)(2,1)} %wo.1), custom_call_target="tpu_custom_call" | custom-call | tf_op jit(solution)/shard_map/sublayer/pallas_call | solution.py:563
  75.8 1.0 %copy.9 = bf16[256,2048]{1,0:T(8,128)(2,1)} copy(bf16[256,2048]{1,0:T(8,128)(2,1)S(1)} %sublayer.1) | data formatting | bytes 2097152
